TPU v7x, 32 devices: a whole 2x2x4 slice. The times are simulated.
32 devices in a mesh: mem: 16 (over z, y, x), patch: 2 (over core).
Axes of the slice: x: 2, y: 2, z: 4, core: 2. Of those that a mesh axis runs over, the one named last changes fastest.
Arguments:
- state: bfloat16 [3, 1024, 8192], P(None, 'mem', 'patch'), may hold values from -6 to 6
- obs_noise: bfloat16 [1024, 8192], P('mem', 'patch'), may hold values from -6 to 6
- obs_values: float32 [2, 4096], P('patch', 'mem'), may hold values from -6 to 6
- obs_weights: bfloat16 [2, 32, 128, 128], P('patch', 'mem'), may hold values from -1 to 1
- tapers: float32 [8, 128, 128], replicated, may hold values from 0.2 to 1
- pair_source: int32 [2, 32, 4], P('patch', 'mem'), may hold values from 0 to 31, as said below
- pair_taper: int32 [2, 32, 4], P('patch', 'mem'), may hold values from 0 to 7
Outputs:
- analysis: bfloat16 [3, 1024, 8192], P(None, 'mem', 'patch')
Inputs may be any that keep to these rules, and one draw needn't show every extreme that they name: `pair_source`: each listed source lies in the same patch within 2 blocks of its target block; positions beyond the patch's ends are moved to its first or last block.
All inputs are finite; a program needn't handle non-finite values.
Results may differ from a plain program's by a relative error of at most 0.0058.
Values may be sent and summed in bfloat16 or wider, within the bound.
A program may use at most 64 MiB of HBM per device.

v0:
```python
import jax
import jax.numpy as jnp
from jax import lax
from jax.sharding import PartitionSpec as P

MEMBERS = 1024
VARIABLES = 3
BLOCK_CELLS = 128
RADIUS = 2
PAIRS = 4
BLOCKS_DEV = 2


def padded(cells, sides, width):
    for axis, dim in sides:
        count = lax.axis_size(axis)
        ends = count - 1
        head = lax.slice_in_dim(cells, 0, width, axis=dim)
        tail = lax.slice_in_dim(cells, cells.shape[dim] - width, cells.shape[dim], axis=dim)
        cells = jnp.concatenate(
            [
                lax.ppermute(tail, axis, [(i, (i + 1) % count) for i in range(ends)]),
                cells,
                lax.ppermute(head, axis, [((i + 1) % count, i) for i in range(ends)]),
            ],
            axis=dim,
        )
    return cells


def centered(values):
    wide = values.astype(jnp.float32)
    return (wide - jnp.mean(wide, axis=-2, keepdims=True)).astype(jnp.bfloat16)


def on_device(state, obs_noise, obs_values, obs_weights, tapers, pair_source, pair_taper):
    observed, noise_cols = (
        lax.all_to_all(state[0], "mem", split_axis=1, concat_axis=0, tiled=True),
        lax.all_to_all(obs_noise, "mem", split_axis=1, concat_axis=0, tiled=True),
    )
    members = observed.shape[0]
    owned = observed.shape[1]
    anom_first = centered(observed)
    innovation = (
        obs_values[0][None, :] + noise_cols.astype(jnp.float32) - observed.astype(jnp.float32)
    ).astype(jnp.bfloat16)
    weighted = jnp.einsum(
        "nkd,kcd->nkc",
        innovation.reshape(members, BLOCKS_DEV, BLOCK_CELLS),
        obs_weights[0],
        preferred_element_type=jnp.float32,
    )
    weighted = weighted.astype(jnp.bfloat16).reshape(members, owned)
    window = padded(jnp.stack([anom_first, weighted]), (("mem", 2),), RADIUS * BLOCK_CELLS)
    others = lax.all_to_all(state[1:], "mem", split_axis=2, concat_axis=1, tiled=True)
    cell_state = jnp.concatenate([observed[None], others], axis=0)
    anomalies = jnp.concatenate([anom_first[None], centered(others)], axis=0)
    first_block = lax.axis_index("mem") * BLOCKS_DEV
    results = []
    for block in range(BLOCKS_DEV):
        target_anom = anomalies[:, :, block * BLOCK_CELLS : (block + 1) * BLOCK_CELLS]
        slices = []
        taper_tiles = []
        for slot in range(PAIRS):
            offset = (pair_source[0, block, slot] - first_block + RADIUS) * BLOCK_CELLS
            slices.append(lax.dynamic_slice_in_dim(window, offset, BLOCK_CELLS, 2))
            taper_tiles.append(
                lax.dynamic_index_in_dim(tapers, pair_taper[0, block, slot], 0, keepdims=False)
            )
        sources = jnp.concatenate(slices, axis=2)
        taper_row = jnp.concatenate(taper_tiles, axis=1)
        pieces = []
        for variable in range(VARIABLES):
            covariance = lax.dot_general(
                target_anom[variable],
                sources[0],
                (((0,), (0,)), ((), ())),
                preferred_element_type=jnp.float32,
            ) / (MEMBERS - 1)
            localized = (taper_row * covariance).astype(jnp.bfloat16)
            pieces.append(
                lax.dot_general(
                    sources[1],
                    localized,
                    (((1,), (1,)), ((), ())),
                    preferred_element_type=jnp.float32,
                )
            )
        total = jnp.stack(pieces)
        results.append(total)
    increment = jnp.concatenate(results, axis=2)
    updated = (cell_state.astype(jnp.float32) + increment).astype(jnp.bfloat16)
    return lax.all_to_all(updated, "mem", split_axis=1, concat_axis=2, tiled=True)


def solution(mesh):
    placed = (
        P(None, "mem", "patch"),
        P("mem", "patch"),
        P("patch", "mem"),
        P("patch", "mem", None, None),
        P(),
        P("patch", "mem", None),
        P("patch", "mem", None),
    )
    return jax.shard_map(
        on_device, mesh=mesh, in_specs=placed, out_specs=P(None, "mem", "patch"), check_vma=False
    )
```

profile of v0, /device:TPU:0, one launch (start us, length us, event | category | flops | bytes accessed | tf_op | source)
XLA Modules:
  0.0 197.0 jit_solution(13814769640638829721)
XLA Ops:
  0.0 1.1 slice.106
  2.2 8.3 %all-to-all-start = ((bf16[64,16,256]{2,0,1:T(8,128)(2,1)}), bf16[64,16,256]{2,0,1:T(8,128)(2,1)S(1)}, u32[]{:S(2)}, u32[]{:S(2)}) async-start(bf16[64,16,256]{2,0,1:T(8,128)(2,1)} %copy.27), calls=%async_computation | async-start | bytes 1048576 | tf_op jit(solution)/shard_map/all_to_all | solution.py:38
  11.4 14.2 %all-to-all-done = bf16[64,16,256]{2,0,1:T(8,128)(2,1)S(1)} async-done(((bf16[64,16,256]{2,0,1:T(8,128)(2,1)}), bf16[64,16,256]{2,0,1:T(8,128)(2,1)S(1)}, u32[]{:S(2)}, u32[]{:S(2)}) %all-to-all-start) | async-done | bytes 524320 | tf_op jit(solution)/shard_map/all_to_all | solution.py:38
  25.7 3.9 %all-to-all-start.2 = ((bf16[64,16,256]{2,0,1:T(8,128)(2,1)}), bf16[64,16,256]{2,0,1:T(8,128)(2,1)S(1)}, u32[]{:S(2)}, u32[]{:S(2)}) async-start(bf16[64,16,256]{2,0,1:T(8,128)(2,1)} %bitcast.130), calls=%async_computation.2 | async-start | bytes 1048576 | tf_op jit(solution)/shard_map/all_to_all | solution.py:39
  30.7 5.0 %copy.41 = bf16[2,64,4096]{1,0,2:T(2,128)(2,1)S(1)} copy(bf16[2,64,4096]{2,1,0:T(8,128)(2,1)} %slice.107) | data formatting | bytes 2097152
  35.7 2.3 %reshape.67 = bf16[16,2,16384]{2,1,0:T(2,128)(2,1)} reshape(bf16[4096,2,64]{2,1,0:T(2,128)(2,1)S(1)} %bitcast.135) | data formatting | bytes 2097152
  38.0 6.1 %all-to-all-done.2 = bf16[64,16,256]{2,0,1:T(8,128)(2,1)S(1)} async-done(((bf16[64,16,256]{2,0,1:T(8,128)(2,1)}), bf16[64,16,256]{2,0,1:T(8,128)(2,1)S(1)}, u32[]{:S(2)}, u32[]{:S(2)}) %all-to-all-start.2) | async-done | bytes 524320 | tf_op jit(solution)/shard_map/all_to_all | solution.py:39
  44.8 3.9 %all-to-all-start.1 = ((bf16[16,2,16384]{2,1,0:T(2,128)(2,1)}), bf16[16,2,16384]{2,1,0:T(2,128)(2,1)S(1)}, u32[]{:S(2)}, u32[]{:S(2)}) async-start(bf16[16,2,16384]{2,1,0:T(2,128)(2,1)} %reshape.67), calls=%async_computation.1 | async-start | bytes 2097152 | tf_op jit(solution)/shard_map/all_to_all | solution.py:55
  48.7 1.1 bitcast_convert_fusion
  49.8 1.7 reshape.66
  52.7 2.7 %reshape.65 = f32[1024,2,128]{2,1,0:T(2,128)} reshape(f32[16,64,256]{2,1,0:T(8,128)} %convert_bitcast_fusion) | data formatting | bytes 2097152 | tf_op jit(solution)/shard_map/convert_element_type | solution.py:45
  55.4 1.8 subtract_convert_fusion.1
  59.9 1.3 collective-permute-start.1
  61.2 5.5 %collective-permute-start = (bf16[2,1024,256]{2,1,0:T(8,128)(2,1)}, bf16[2,1024,256]{2,1,0:T(8,128)(2,1)}, u32[]{:S(2)}, u32[]{:S(2)}) collective-permute-start(bf16[2,1024,256]{2,1,0:T(8,128)(2,1)} %pad_maximum_fusion.3), channel_id=1, source_target_pairs={{0,2},{2,4},{4,6},{6,8},{8,10},{10,12},{12,14},{14,16},{16,18},{18... | collective-permute-start | bytes 3145736 | tf_op jit(solution)/shard_map/ppermute | solution.py:22
  89.6 1.3 reshape.68
  91.0 2.4 %copy.39 = bf16[2,64,16,256]{3,2,1,0:T(8,128)(2,1)} copy(bf16[2,64,16,256]{1,0,3,2:T(2,128)(2,1)S(1)} %bitcast.131) | data formatting | bytes 2097152 | tf_op jit(solution)/shard_map/all_to_all | solution.py:55
  93.3 1.4 copy.40
  94.8 1.3 copy.32
  96.3 1.3 subtract_convert_fusion
  97.6 14.6 %collective-permute-done = bf16[2,1024,256]{2,1,0:T(8,128)(2,1)} collective-permute-done((bf16[2,1024,256]{2,1,0:T(8,128)(2,1)}, bf16[2,1024,256]{2,1,0:T(8,128)(2,1)}, u32[]{:S(2)}, u32[]{:S(2)}) %collective-permute-start) | collective-permute-done | bytes 1048608 | tf_op jit(solution)/shard_map/ppermute | solution.py:22
  112.2 1.6 pad_maximum_fusion
  114.8 1.6 pad_maximum_fusion.1
  116.4 3.1 %convolution_bitcast_fusion = f32[1,1024,128]{1,2,0:T(8,128)S(1)} fusion(bf16[2,1024,512]{2,1,0:T(8,128)(2,1)} %get-tuple-element.38, bf16[2,1024,256]{2,1,0:T(8,128)(2,1)} %subtract_convert_fusion, f32[128,128]{1,0:T(8,128)} %get-tuple-element.19, f32[128,128]{1,0:T(8,128)} %get-tuple-element.20, f32[128,128]{1,0:T(8,128)S(1)} %get-tuple-element.14, ...), kind=kOutput, calls=%fused_computation.8 | convolution fusion | flops 268828672 | bytes 3145728 | tf_op jit(solution)/shard_map/dot_general | solution.py:82
  119.5 3.2 %convolution_bitcast_fusion.1 = f32[1,1024,128]{1,2,0:T(8,128)} fusion(bf16[2,1024,512]{2,1,0:T(8,128)(2,1)} %get-tuple-element.38, bf16[2,1024,256]{2,1,0:T(8,128)(2,1)} %subtract_convert_fusion, f32[128,128]{1,0:T(8,128)} %get-tuple-element.19, f32[128,128]{1,0:T(8,128)} %get-tuple-element.20, f32[128,128]{1,0:T(8,128)S(1)} %get-tuple-element.14, ...), kind=kOutput, calls=%fused_computation.9 | convolution fusion | flops 268828672 | bytes 3145728 | tf_op jit(solution)/shard_map/dot_general | solution.py:82
  122.7 3.1 %convolution_bitcast_fusion.2 = f32[1,1024,128]{1,2,0:T(8,128)} fusion(bf16[2,1024,512]{2,1,0:T(8,128)(2,1)} %get-tuple-element.38, bf16[1,1024,256]{2,1,0:T(8,128)(2,1)S(1)} %copy-done.2, f32[128,128]{1,0:T(8,128)} %get-tuple-element.19, f32[128,128]{1,0:T(8,128)} %get-tuple-element.20, f32[128,128]{1,0:T(8,128)S(1)} %get-tuple-element.14, ...), kind=kOutput, calls=%fused_computation.10 | convolution fusion | flops 268828672 | bytes 3145728 | tf_op jit(solution)/shard_map/dot_general | solution.py:82
  125.8 2.5 %convolution_bitcast_fusion.3 = f32[1,1024,128]{1,2,0:T(8,128)} fusion(bf16[2,1024,512]{2,1,0:T(8,128)(2,1)S(1)} %get-tuple-element.37, bf16[2,1024,256]{2,1,0:T(8,128)(2,1)} %subtract_convert_fusion, f32[128,128]{1,0:T(8,128)S(1)} %get-tuple-element.16, f32[128,128]{1,0:T(8,128)S(1)} %get-tuple-element.17, f32[128,128]{1,0:T(8,128)S(1)} %get-tuple-element.18, ...), kind=kOutput, calls=%fused_computation.11 | convolution fusion | flops 268828672 | bytes 3145728 | tf_op jit(solution)/shard_map/dot_general | solution.py:82
  128.2 2.5 %convolution_bitcast_fusion.4 = f32[1,1024,128]{1,2,0:T(8,128)} fusion(bf16[2,1024,512]{2,1,0:T(8,128)(2,1)S(1)} %get-tuple-element.37, bf16[2,1024,256]{2,1,0:T(8,128)(2,1)} %subtract_convert_fusion, f32[128,128]{1,0:T(8,128)S(1)} %get-tuple-element.16, f32[128,128]{1,0:T(8,128)S(1)} %get-tuple-element.17, f32[128,128]{1,0:T(8,128)S(1)} %get-tuple-element.18, ...), kind=kOutput, calls=%fused_computation.12 | convolution fusion | flops 268828672 | bytes 3145728 | tf_op jit(solution)/shard_map/dot_general | solution.py:82
  130.7 3.2 %convolution_bitcast_fusion.5 = f32[1,1024,128]{1,2,0:T(8,128)} fusion(bf16[2,1024,512]{2,1,0:T(8,128)(2,1)} %copy-done.10, bf16[1,1024,256]{2,1,0:T(8,128)(2,1)S(1)} %copy-done.2, f32[128,128]{1,0:T(8,128)S(1)} %get-tuple-element.16, f32[128,128]{1,0:T(8,128)S(1)} %get-tuple-element.17, f32[128,128]{1,0:T(8,128)S(1)} %get-tuple-element.18, ...), kind=kOutput, calls=%fused_computation.13 | convolution fusion | flops 268828672 | bytes 3145728 | tf_op jit(solution)/shard_map/dot_general | solution.py:82
  133.9 2.7 %fusion = bf16[3,1024,256]{1,2,0:T(8,128)(2,1)} fusion(f32[1,1024,128]{1,2,0:T(8,128)S(1)} %convolution_bitcast_fusion, f32[1,1024,128]{1,2,0:T(8,128)S(1)} %copy-done.12, f32[1,1024,128]{1,2,0:T(8,128)} %convolution_bitcast_fusion.2, f32[1,1024,128]{1,2,0:T(8,128)} %convolution_bitcast_fusion.3, f32[1,1024,128]{1,2,0:T(8,128)} %convolution_bitcast_fusion.4, ...), kind=kLoop, calls=%fused_computation.2 | loop fusion | flops 7077888 | bytes 6291456 | tf_op jit(solution)/shard_map/convert_element_type | solution.py:92
  136.6 2.9 %copy.36 = bf16[3,1024,256]{2,0,1:T(4,128)(2,1)S(1)} copy(bf16[3,1024,256]{1,2,0:T(8,128)(2,1)} %fusion) | data formatting | bytes 3145728 | tf_op jit(solution)/shard_map/convert_element_type | solution.py:92
  139.6 55.9 %all_to_all.65 = bf16[3,1024,256]{2,0,1:T(4,128)(2,1)S(1)} all-to-all(bf16[3,1024,256]{2,0,1:T(4,128)(2,1)S(1)} %copy.36), channel_id=1, replica_groups=mesh['mem'=16,'patch'=2] {'mem'}, dimensions={1} | all-to-all | bytes 3145728 | tf_op jit(solution)/shard_map/all_to_all | solution.py:93
  195.7 1.3 copy.43
  (57 shorter events, 12.0 us)
Async XLA Ops:
  0.0 57.1 %copy-start = (bf16[1,2,128,128]{3,2,1,0:T(8,128)(2,1)S(1)}, bf16[1,2,128,128]{3,2,1,0:T(8,128)(2,1)}, u32[]{:S(2)}) copy-start(bf16[1,2,128,128]{3,2,1,0:T(8,128)(2,1)} %param.10) | copy-start | bytes 196612
  0.0 10.6 %copy-start.13 = (bf16[64,4096]{1,0:T(8,128)(2,1)S(1)}, bf16[64,4096]{1,0:T(8,128)(2,1)}, u32[]{:S(2)}) copy-start(bf16[64,4096]{1,0:T(8,128)(2,1)} %param.8) | copy-start | bytes 1572868
  1.3 28.4 %copy-start.11 = (bf16[3,64,4096]{2,1,0:T(8,128)(2,1)S(1)}, bf16[3,64,4096]{2,1,0:T(8,128)(2,1)}, u32[]{:S(2)}) copy-start(bf16[3,64,4096]{2,1,0:T(8,128)(2,1)} %param.7) | copy-start | bytes 4718596
  2.2 23.4 %all-to-all-start = ((bf16[64,16,256]{2,0,1:T(8,128)(2,1)}), bf16[64,16,256]{2,0,1:T(8,128)(2,1)S(1)}, u32[]{:S(2)}, u32[]{:S(2)}) async-start(bf16[64,16,256]{2,0,1:T(8,128)(2,1)} %copy.27), calls=%async_computation | async-start | bytes 1048576 | tf_op jit(solution)/shard_map/all_to_all | solution.py:38
  25.7 18.4 %all-to-all-start.2 = ((bf16[64,16,256]{2,0,1:T(8,128)(2,1)}), bf16[64,16,256]{2,0,1:T(8,128)(2,1)S(1)}, u32[]{:S(2)}, u32[]{:S(2)}) async-start(bf16[64,16,256]{2,0,1:T(8,128)(2,1)} %bitcast.130), calls=%async_computation.2 | async-start | bytes 1048576 | tf_op jit(solution)/shard_map/all_to_all | solution.py:39
  44.0 0.8 copy-start.8
  44.8 44.8 %all-to-all-start.1 = ((bf16[16,2,16384]{2,1,0:T(2,128)(2,1)}), bf16[16,2,16384]{2,1,0:T(2,128)(2,1)S(1)}, u32[]{:S(2)}, u32[]{:S(2)}) async-start(bf16[16,2,16384]{2,1,0:T(2,128)(2,1)} %reshape.67), calls=%async_computation.1 | async-start | bytes 2097152 | tf_op jit(solution)/shard_map/all_to_all | solution.py:55
  48.7 2.8 %copy-start.9 = (bf16[64,16,256]{2,0,1:T(8,128)(2,1)S(1)}, bf16[64,16,256]{2,0,1:T(8,128)(2,1)}, u32[]{:S(2)}) copy-start(bf16[64,16,256]{2,0,1:T(8,128)(2,1)} %copy-done.8) | copy-start | bytes 1572868
  51.6 3.8 %copy-start.17 = (f32[1,256]{1,0:T(1,128)S(1)}, f32[1,256]{1,0:T(1,128)}, u32[]{:S(2)}) copy-start(f32[1,256]{1,0:T(1,128)} %param.9) | copy-start | bytes 3076
  57.7 30.9 %copy-start.3 = (bf16[1,1024,256]{2,1,0:T(8,128)(2,1)}, bf16[1,1024,256]{2,1,0:T(8,128)(2,1)S(1)}, u32[]{:S(2)}) copy-start(bf16[1,1024,256]{2,1,0:T(8,128)(2,1)S(1)} %copy.35) | copy-start | bytes 1572868
  57.7 9.0 %copy-start.15 = (s32[1,2,4]{2,1,0:T(2,128)S(1)}, s32[1,2,4]{2,1,0:T(2,128)}, u32[]{:S(2)}) copy-start(s32[1,2,4]{2,1,0:T(2,128)} %param.12) | copy-start | bytes 100
  57.7 14.7 %copy-start.16 = (s32[1,2,4]{2,1,0:T(2,128)S(1)}, s32[1,2,4]{2,1,0:T(2,128)}, u32[]{:S(2)}) copy-start(s32[1,2,4]{2,1,0:T(2,128)} %param.13) | copy-start | bytes 100
  57.7 30.2 %copy-start.14 = (f32[8,128,128]{2,1,0:T(8,128)S(1)}, f32[8,128,128]{2,1,0:T(8,128)}, u32[]{:S(2)}) copy-start(f32[8,128,128]{2,1,0:T(8,128)} %param.11) | copy-start | bytes 1572868
  58.0 0.8 copy-start.1
  59.9 37.7 %collective-permute-start.1 = (bf16[2,1024,256]{2,1,0:T(8,128)(2,1)}, bf16[2,1024,256]{2,1,0:T(8,128)(2,1)}, u32[]{:S(2)}, u32[]{:S(2)}) collective-permute-start(bf16[2,1024,256]{2,1,0:T(8,128)(2,1)} %pad_maximum_fusion.3), channel_id=1, source_target_pairs={{2,0},{4,2},{6,4},{8,6},{10,8},{12,10},{14,12},{16,14},{18,16},{20... | collective-permute-start | bytes 3145736 | tf_op jit(solution)/shard_map/ppermute | solution.py:24
  61.2 51.1 %collective-permute-start = (bf16[2,1024,256]{2,1,0:T(8,128)(2,1)}, bf16[2,1024,256]{2,1,0:T(8,128)(2,1)}, u32[]{:S(2)}, u32[]{:S(2)}) collective-permute-start(bf16[2,1024,256]{2,1,0:T(8,128)(2,1)} %pad_maximum_fusion.3), channel_id=1, source_target_pairs={{0,2},{2,4},{4,6},{6,8},{8,10},{10,12},{12,14},{14,16},{16,18},{18... | collective-permute-start | bytes 3145736 | tf_op jit(solution)/shard_map/ppermute | solution.py:22
  94.8 1.3 copy-start.5
  96.1 16.1 %copy-start.2 = (bf16[1,1024,256]{2,1,0:T(8,128)(2,1)S(1)}, bf16[1,1024,256]{2,1,0:T(8,128)(2,1)}, u32[]{:S(2)}) copy-start(bf16[1,1024,256]{2,1,0:T(8,128)(2,1)} %copy-done.1) | copy-start | bytes 1572868
  96.1 16.1 %copy-start.4 = (bf16[1,1024,256]{2,1,0:T(8,128)(2,1)S(1)}, bf16[1,1024,256]{2,1,0:T(8,128)(2,1)}, u32[]{:S(2)}) copy-start(bf16[1,1024,256]{2,1,0:T(8,128)(2,1)} %copy-done.3) | copy-start | bytes 1572868
  116.4 11.9 %copy-start.10 = (bf16[2,1024,512]{2,1,0:T(8,128)(2,1)}, bf16[2,1024,512]{2,1,0:T(8,128)(2,1)S(1)}, u32[]{:S(2)}) copy-start(bf16[2,1024,512]{2,1,0:T(8,128)(2,1)S(1)} %get-tuple-element.37) | copy-start | bytes 6291460
  130.7 3.2 %copy-start.6 = (bf16[2,1024,256]{1,2,0:T(8,128)(2,1)S(1)}, bf16[2,1024,256]{1,2,0:T(8,128)(2,1)}, u32[]{:S(2)}) copy-start(bf16[2,1024,256]{1,2,0:T(8,128)(2,1)} %copy.32) | copy-start | bytes 3145732
  130.7 3.2 %copy-start.7 = (bf16[1,1024,256]{1,2,0:T(8,128)(2,1)S(1)}, bf16[1,1024,256]{1,2,0:T(8,128)(2,1)}, u32[]{:S(2)}) copy-start(bf16[1,1024,256]{1,2,0:T(8,128)(2,1)} %copy.31) | copy-start | bytes 1572868
  130.7 3.2 %copy-start.12 = (f32[1,1024,128]{1,2,0:T(8,128)S(1)}, f32[1,1024,128]{1,2,0:T(8,128)}, u32[]{:S(2)}) copy-start(f32[1,1024,128]{1,2,0:T(8,128)} %convolution_bitcast_fusion.1) | copy-start | bytes 1572868
where the time goes:
time: 198 us; the launch traced here: 197 us
  blocking collectives  55.9 us (28%)
  waiting for transfers between devices  34.9 us (18%)
  local copies, waits for them, and re-layouts  32.6 us (16%)
  starting transfers between devices  23 us (12%)
  between operations  20.1 us (10%)
  matrix products  17.8 us (9%)
  other arithmetic  12.7 us (6%)
    all_to_all x1, blocking collectives, on_device(): lax.all_to_all(updated, 'mem', split_axis=1, concat_axis=2, tiled=True)  55.9 us
    dot_general x6, matrix products, on_device(): lax.dot_general(sources[1], localized, (((1,), (1,)), ((), ())), preferre...  17.5 us
    ppermute x1, waiting for transfers between devices, padded(): lax.ppermute(tail, axis, [(i, (i + 1) % count) for i in range(ends)])  14.6 us
    all_to_all x1, waiting for transfers between devices, on_device(): lax.all_to_all(state[0], 'mem', split_axis=1, concat_axis=0, tiled=True)  14.2 us
    unnamed x40, local copies, waits for them, and re-layouts  10.4 us
    all_to_all x1, starting transfers between devices, on_device(): lax.all_to_all(state[0], 'mem', split_axis=1, concat_axis=0, tiled=True)  8.34 us
    all_to_all x1, waiting for transfers between devices, on_device(): lax.all_to_all(obs_noise, 'mem', split_axis=1, concat_axis=0, tiled=True)  6.07 us
    ppermute x1, starting transfers between devices, padded(): lax.ppermute(tail, axis, [(i, (i + 1) % count) for i in range(ends)])  5.55 us
  transfers between devices with their start and end apart: 5, of which 3 were waited for; matrix products, arithmetic and copies ran while one was open for 15% of the time, Pallas kernels for 0%

commit v1 on v0

--- a/solution.py
+++ b/solution.py
@@ -90,7 +90,15 @@
         results.append(total)
     increment = jnp.concatenate(results, axis=2)
     updated = (cell_state.astype(jnp.float32) + increment).astype(jnp.bfloat16)
-    return lax.all_to_all(updated, "mem", split_axis=1, concat_axis=2, tiled=True)
+    return jnp.concatenate(
+        lax.all_to_all(
+            jnp.stack(jnp.split(updated, lax.axis_size("mem"), axis=1), axis=0),
+            axis_name="mem",
+            split_axis=0,
+            concat_axis=0,
+        ),
+        axis=2,
+    )
 
 
 def solution(mesh):

time: 198 us -> 200 us (1.010)
  local copies, waits for them, and re-layouts: 32.6 us -> 44.2 us
  blocking collectives: 55.9 us -> 44.7 us
    unnamed x40 -> x59, local copies, waits for them, and re-layouts: 10.4 us -> 21.8 us
    all_to_all x1, blocking collectives: 55.9 us -> 44.7 us  [on_device(): lax.all_to_all(jnp.stack(jnp.split(updated, lax.axis_size('mem'), axis=1)...]
    another operation x0 -> x2, local copies, waits for them, and re-layouts: none -> 3.95 us  [on_device(): jnp.stack(jnp.split(updated, lax.axis_size('mem'), axis=1), axis=0)]
    convert_element_type x1 -> x0, local copies, waits for them, and re-layouts: 2.93 us -> none  [on_device(): updated = (cell_state.astype(jnp.float32) + increment).astype(jnp.bfloat16)]
  transfers between devices with their start and end apart: 5 -> 5, of which waited for: 3 -> 3; matrix products, arithmetic and copies ran while one was open for 15% -> 16% of each run, Pallas kernels for 0% -> 0%
where the time goes in v1:
time: 200 us; the launch traced here: 199 us
  blocking collectives  44.7 us (22%)
  local copies, waits for them, and re-layouts  44.2 us (22%)
  waiting for transfers between devices  34.5 us (17%)
  starting transfers between devices  23 us (12%)
  between operations  20 us (10%)
  matrix products  18.8 us (9%)
  other arithmetic  13.7 us (7%)
    all_to_all x1, blocking collectives, on_device(): lax.all_to_all(jnp.stack(jnp.split(updated, lax.axis_size('mem'), axis=1)...  44.7 us
    unnamed x59, local copies, waits for them, and re-layouts  21.8 us
    dot_general x6, matrix products, on_device(): lax.dot_general(sources[1], localized, (((1,), (1,)), ((), ())), preferre...  18.5 us
    ppermute x1, waiting for transfers between devices, padded(): lax.ppermute(tail, axis, [(i, (i + 1) % count) for i in range(ends)])  14.2 us
    all_to_all x1, waiting for transfers between devices, on_device(): lax.all_to_all(state[0], 'mem', split_axis=1, concat_axis=0, tiled=True)  14.2 us
    all_to_all x1, starting transfers between devices, on_device(): lax.all_to_all(state[0], 'mem', split_axis=1, concat_axis=0, tiled=True)  8.35 us
    all_to_all x1, waiting for transfers between devices, on_device(): lax.all_to_all(obs_noise, 'mem', split_axis=1, concat_axis=0, tiled=True)  6.06 us
    ppermute x1, starting transfers between devices, padded(): lax.ppermute(tail, axis, [(i, (i + 1) % count) for i in range(ends)])  5.55 us
  transfers between devices with their start and end apart: 5, of which 3 were waited for; matrix products, arithmetic and copies ran while one was open for 16% of the time, Pallas kernels for 0%

profile of v1, /device:TPU:0, one launch (start us, length us, event | category | flops | bytes accessed | tf_op | source)
XLA Modules:
  0.0 199.0 jit_solution(13300548634512912683)
XLA Ops:
  0.0 1.2 slice.106
  2.3 8.3 %all-to-all-start = ((bf16[64,16,256]{2,0,1:T(8,128)(2,1)}), bf16[64,16,256]{2,0,1:T(8,128)(2,1)S(1)}, u32[]{:S(2)}, u32[]{:S(2)}) async-start(bf16[64,16,256]{2,0,1:T(8,128)(2,1)} %copy.25), calls=%async_computation | async-start | bytes 1048576 | tf_op jit(solution)/shard_map/all_to_all | solution.py:38
  11.5 14.2 %all-to-all-done = bf16[64,16,256]{2,0,1:T(8,128)(2,1)S(1)} async-done(((bf16[64,16,256]{2,0,1:T(8,128)(2,1)}), bf16[64,16,256]{2,0,1:T(8,128)(2,1)S(1)}, u32[]{:S(2)}, u32[]{:S(2)}) %all-to-all-start) | async-done | bytes 524320 | tf_op jit(solution)/shard_map/all_to_all | solution.py:38
  25.7 3.9 %all-to-all-start.2 = ((bf16[64,16,256]{2,0,1:T(8,128)(2,1)}), bf16[64,16,256]{2,0,1:T(8,128)(2,1)S(1)}, u32[]{:S(2)}, u32[]{:S(2)}) async-start(bf16[64,16,256]{2,0,1:T(8,128)(2,1)} %bitcast.192), calls=%async_computation.2 | async-start | bytes 1048576 | tf_op jit(solution)/shard_map/all_to_all | solution.py:39
  30.7 5.0 %copy.38 = bf16[2,64,4096]{1,0,2:T(2,128)(2,1)S(1)} copy(bf16[2,64,4096]{2,1,0:T(8,128)(2,1)} %slice.107) | data formatting | bytes 2097152
  35.8 2.3 %reshape.75 = bf16[16,2,16384]{2,1,0:T(2,128)(2,1)} reshape(bf16[4096,2,64]{2,1,0:T(2,128)(2,1)S(1)} %bitcast.197) | data formatting | bytes 2097152
  38.0 6.1 %all-to-all-done.2 = bf16[64,16,256]{2,0,1:T(8,128)(2,1)S(1)} async-done(((bf16[64,16,256]{2,0,1:T(8,128)(2,1)}), bf16[64,16,256]{2,0,1:T(8,128)(2,1)S(1)}, u32[]{:S(2)}, u32[]{:S(2)}) %all-to-all-start.2) | async-done | bytes 524320 | tf_op jit(solution)/shard_map/all_to_all | solution.py:39
  44.9 3.9 %all-to-all-start.1 = ((bf16[16,2,16384]{2,1,0:T(2,128)(2,1)}), bf16[16,2,16384]{2,1,0:T(2,128)(2,1)S(1)}, u32[]{:S(2)}, u32[]{:S(2)}) async-start(bf16[16,2,16384]{2,1,0:T(2,128)(2,1)} %reshape.75), calls=%async_computation.1 | async-start | bytes 2097152 | tf_op jit(solution)/shard_map/all_to_all | solution.py:55
  48.8 1.1 bitcast_convert_fusion
  49.9 1.8 reshape.74
  52.7 2.7 %reshape.73 = f32[1024,2,128]{2,1,0:T(2,128)} reshape(f32[16,64,256]{2,1,0:T(8,128)} %convert_bitcast_fusion) | data formatting | bytes 2097152 | tf_op jit(solution)/shard_map/convert_element_type | solution.py:45
  55.4 1.8 subtract_convert_fusion.1
  59.9 1.3 collective-permute-start.1
  61.2 5.6 %collective-permute-start = (bf16[2,1024,256]{2,1,0:T(8,128)(2,1)}, bf16[2,1024,256]{2,1,0:T(8,128)(2,1)}, u32[]{:S(2)}, u32[]{:S(2)}) collective-permute-start(bf16[2,1024,256]{2,1,0:T(8,128)(2,1)} %pad_maximum_fusion.3), channel_id=1, source_target_pairs={{0,2},{2,4},{4,6},{6,8},{8,10},{10,12},{12,14},{14,16},{16,18},{18... | collective-permute-start | bytes 3145736 | tf_op jit(solution)/shard_map/ppermute | solution.py:22
  89.6 1.3 reshape.76
  90.9 2.4 %copy.36 = bf16[2,64,16,256]{3,2,1,0:T(8,128)(2,1)} copy(bf16[2,64,16,256]{1,0,3,2:T(2,128)(2,1)S(1)} %bitcast.193) | data formatting | bytes 2097152 | tf_op jit(solution)/shard_map/all_to_all | solution.py:55
  93.3 1.4 copy.37
  95.3 1.4 convert_reduce_fusion
  96.8 1.3 subtract_convert_fusion
  98.1 14.2 %collective-permute-done = bf16[2,1024,256]{2,1,0:T(8,128)(2,1)} collective-permute-done((bf16[2,1024,256]{2,1,0:T(8,128)(2,1)}, bf16[2,1024,256]{2,1,0:T(8,128)(2,1)}, u32[]{:S(2)}, u32[]{:S(2)}) %collective-permute-start) | collective-permute-done | bytes 1048608 | tf_op jit(solution)/shard_map/ppermute | solution.py:22
  112.3 1.6 pad_maximum_fusion
  114.9 2.2 %pad_maximum_fusion.1 = (bf16[2,1024,512]{2,1,0:T(8,128)(2,1)}, bf16[2,1024,512]{2,1,0:T(8,128)(2,1)}) fusion(bf16[2,1024,128]{2,1,0:T(8,128)(2,1)S(1)} %get-tuple-element.10, bf16[2,1024,128]{2,1,0:T(8,128)(2,1)S(1)} %get-tuple-element.11, bf16[2,1024,128]{2,1,0:T(8,128)(2,1)S(1)} %get-tuple-element.12, bf16[2,1024,128]{2,1,0:T(8,128)(2,1)S(1)} %get-tuple-element.5, ...), kind=kLoop, calls=%fused_computation.3 | loop fusion | flops 16777216 | bytes 8388608 | tf_op jit(solution)/shard_map/concatenate | solution.py:70
  117.1 3.1 %convolution_bitcast_fusion = f32[1,1024,128]{1,2,0:T(8,128)} fusion(bf16[2,1024,512]{2,1,0:T(8,128)(2,1)} %get-tuple-element.38, bf16[2,1024,256]{2,1,0:T(8,128)(2,1)S(1)} %copy-done.9, f32[128,128]{1,0:T(8,128)} %get-tuple-element.19, f32[128,128]{1,0:T(8,128)} %get-tuple-element.20, f32[128,128]{1,0:T(8,128)S(1)} %get-tuple-element.14, ...), kind=kOutput, calls=%fused_computation.8 | convolution fusion | flops 268828672 | bytes 3145728 | tf_op jit(solution)/shard_map/dot_general | solution.py:82
  120.2 3.1 %convolution_bitcast_fusion.1 = f32[1,1024,128]{1,2,0:T(8,128)} fusion(bf16[2,1024,512]{2,1,0:T(8,128)(2,1)} %get-tuple-element.38, bf16[2,1024,256]{2,1,0:T(8,128)(2,1)S(1)} %copy-done.9, f32[128,128]{1,0:T(8,128)S(1)} %copy-done.15, f32[128,128]{1,0:T(8,128)S(1)} %copy-done.16, f32[128,128]{1,0:T(8,128)S(1)} %get-tuple-element.14, ...), kind=kOutput, calls=%fused_computation.9 | convolution fusion | flops 268828672 | bytes 3145728 | tf_op jit(solution)/shard_map/dot_general | solution.py:82
  123.3 3.1 %convolution_bitcast_fusion.2 = f32[1,1024,128]{1,2,0:T(8,128)} fusion(bf16[2,1024,512]{2,1,0:T(8,128)(2,1)} %get-tuple-element.38, bf16[1,1024,256]{2,1,0:T(8,128)(2,1)S(1)} %copy-done.2, f32[128,128]{1,0:T(8,128)S(1)} %copy-done.15, f32[128,128]{1,0:T(8,128)S(1)} %copy-done.16, f32[128,128]{1,0:T(8,128)S(1)} %get-tuple-element.14, ...), kind=kOutput, calls=%fused_computation.10 | convolution fusion | flops 268828672 | bytes 3145728 | tf_op jit(solution)/shard_map/dot_general | solution.py:82
  126.3 3.1 %convolution_bitcast_fusion.3 = f32[1,1024,128]{1,2,0:T(8,128)} fusion(bf16[2,1024,512]{2,1,0:T(8,128)(2,1)} %get-tuple-element.37, bf16[2,1024,256]{2,1,0:T(8,128)(2,1)S(1)} %copy-done.9, f32[128,128]{1,0:T(8,128)S(1)} %get-tuple-element.16, f32[128,128]{1,0:T(8,128)S(1)} %get-tuple-element.17, f32[128,128]{1,0:T(8,128)S(1)} %get-tuple-element.18, ...), kind=kOutput, calls=%fused_computation.11 | convolution fusion | flops 268828672 | bytes 3145728 | tf_op jit(solution)/shard_map/dot_general | solution.py:82
  129.4 3.1 %convolution_bitcast_fusion.4 = f32[1,1024,128]{1,2,0:T(8,128)} fusion(bf16[2,1024,512]{2,1,0:T(8,128)(2,1)} %get-tuple-element.37, bf16[2,1024,256]{2,1,0:T(8,128)(2,1)S(1)} %copy-done.9, f32[128,128]{1,0:T(8,128)S(1)} %get-tuple-element.16, f32[128,128]{1,0:T(8,128)S(1)} %get-tuple-element.17, f32[128,128]{1,0:T(8,128)S(1)} %get-tuple-element.18, ...), kind=kOutput, calls=%fused_computation.12 | convolution fusion | flops 268828672 | bytes 3145728 | tf_op jit(solution)/shard_map/dot_general | solution.py:82
  132.5 3.1 %convolution_bitcast_fusion.5 = f32[1,1024,128]{1,2,0:T(8,128)} fusion(bf16[2,1024,512]{2,1,0:T(8,128)(2,1)} %get-tuple-element.37, bf16[1,1024,256]{2,1,0:T(8,128)(2,1)S(1)} %copy-done.2, f32[128,128]{1,0:T(8,128)S(1)} %get-tuple-element.16, f32[128,128]{1,0:T(8,128)S(1)} %get-tuple-element.17, f32[128,128]{1,0:T(8,128)S(1)} %get-tuple-element.18, ...), kind=kOutput, calls=%fused_computation.13 | convolution fusion | flops 268828672 | bytes 3145728 | tf_op jit(solution)/shard_map/dot_general | solution.py:82
  135.7 1.9 fusion
  149.8 3.1 %copy.34 = bf16[16,3,64,256]{3,2,1,0:T(8,128)(2,1)S(1)} copy(bf16[16,3,64,256]{2,3,1,0:T(8,128)(2,1)} %fusion.15) | data formatting | bytes 3145728 | tf_op jit(solution)/shard_map/stack | solution.py:95
  153.0 44.7 %all_to_all.52 = bf16[16,3,64,256]{3,2,1,0:T(8,128)(2,1)S(1)} all-to-all(bf16[16,3,64,256]{3,2,1,0:T(8,128)(2,1)S(1)} %copy.34), channel_id=1, replica_groups=mesh['mem'=16,'patch'=2] {'mem'}, dimensions={0} | all-to-all | bytes 3145728 | tf_op jit(solution)/shard_map/all_to_all | solution.py:94
  197.6 1.3 copy.40
  (76 shorter events, 24.3 us)
Async XLA Ops:
  0.0 57.2 %copy-start = (bf16[1,2,128,128]{3,2,1,0:T(8,128)(2,1)S(1)}, bf16[1,2,128,128]{3,2,1,0:T(8,128)(2,1)}, u32[]{:S(2)}) copy-start(bf16[1,2,128,128]{3,2,1,0:T(8,128)(2,1)} %param.10) | copy-start | bytes 196612
  0.0 29.7 %copy-start.8 = (bf16[3,64,4096]{2,1,0:T(8,128)(2,1)S(1)}, bf16[3,64,4096]{2,1,0:T(8,128)(2,1)}, u32[]{:S(2)}) copy-start(bf16[3,64,4096]{2,1,0:T(8,128)(2,1)} %param.7) | copy-start | bytes 4718596
  0.0 10.7 %copy-start.12 = (bf16[64,4096]{1,0:T(8,128)(2,1)S(1)}, bf16[64,4096]{1,0:T(8,128)(2,1)}, u32[]{:S(2)}) copy-start(bf16[64,4096]{1,0:T(8,128)(2,1)} %param.8) | copy-start | bytes 1572868
  2.3 23.4 %all-to-all-start = ((bf16[64,16,256]{2,0,1:T(8,128)(2,1)}), bf16[64,16,256]{2,0,1:T(8,128)(2,1)S(1)}, u32[]{:S(2)}, u32[]{:S(2)}) async-start(bf16[64,16,256]{2,0,1:T(8,128)(2,1)} %copy.25), calls=%async_computation | async-start | bytes 1048576 | tf_op jit(solution)/shard_map/all_to_all | solution.py:38
  25.7 18.4 %all-to-all-start.2 = ((bf16[64,16,256]{2,0,1:T(8,128)(2,1)}), bf16[64,16,256]{2,0,1:T(8,128)(2,1)S(1)}, u32[]{:S(2)}, u32[]{:S(2)}) async-start(bf16[64,16,256]{2,0,1:T(8,128)(2,1)} %bitcast.192), calls=%async_computation.2 | async-start | bytes 1048576 | tf_op jit(solution)/shard_map/all_to_all | solution.py:39
  44.1 0.8 copy-start.6
  44.9 44.7 %all-to-all-start.1 = ((bf16[16,2,16384]{2,1,0:T(2,128)(2,1)}), bf16[16,2,16384]{2,1,0:T(2,128)(2,1)S(1)}, u32[]{:S(2)}, u32[]{:S(2)}) async-start(bf16[16,2,16384]{2,1,0:T(2,128)(2,1)} %reshape.75), calls=%async_computation.1 | async-start | bytes 2097152 | tf_op jit(solution)/shard_map/all_to_all | solution.py:55
  48.8 2.9 %copy-start.7 = (bf16[64,16,256]{2,0,1:T(8,128)(2,1)S(1)}, bf16[64,16,256]{2,0,1:T(8,128)(2,1)}, u32[]{:S(2)}) copy-start(bf16[64,16,256]{2,0,1:T(8,128)(2,1)} %copy-done.6) | copy-start | bytes 1572868
  49.9 5.5 %copy-start.19 = (f32[1,256]{1,0:T(1,128)S(1)}, f32[1,256]{1,0:T(1,128)}, u32[]{:S(2)}) copy-start(f32[1,256]{1,0:T(1,128)} %param.9) | copy-start | bytes 3076
  57.2 9.6 %copy-start.17 = (s32[1,2,4]{2,1,0:T(2,128)S(1)}, s32[1,2,4]{2,1,0:T(2,128)}, u32[]{:S(2)}) copy-start(s32[1,2,4]{2,1,0:T(2,128)} %param.12) | copy-start | bytes 100
  57.2 15.2 %copy-start.18 = (s32[1,2,4]{2,1,0:T(2,128)S(1)}, s32[1,2,4]{2,1,0:T(2,128)}, u32[]{:S(2)}) copy-start(s32[1,2,4]{2,1,0:T(2,128)} %param.13) | copy-start | bytes 100
  57.6 30.3 %copy-start.13 = (f32[8,128,128]{2,1,0:T(8,128)S(1)}, f32[8,128,128]{2,1,0:T(8,128)}, u32[]{:S(2)}) copy-start(f32[8,128,128]{2,1,0:T(8,128)} %param.11) | copy-start | bytes 1572868
  57.8 31.8 %copy-start.3 = (bf16[1,1024,256]{2,1,0:T(8,128)(2,1)}, bf16[1,1024,256]{2,1,0:T(8,128)(2,1)S(1)}, u32[]{:S(2)}) copy-start(bf16[1,1024,256]{2,1,0:T(8,128)(2,1)S(1)} %copy.33) | copy-start | bytes 1572868
  58.1 0.8 copy-start.1
  59.9 38.1 %collective-permute-start.1 = (bf16[2,1024,256]{2,1,0:T(8,128)(2,1)}, bf16[2,1024,256]{2,1,0:T(8,128)(2,1)}, u32[]{:S(2)}, u32[]{:S(2)}) collective-permute-start(bf16[2,1024,256]{2,1,0:T(8,128)(2,1)} %pad_maximum_fusion.3), channel_id=1, source_target_pairs={{2,0},{4,2},{6,4},{8,6},{10,8},{12,10},{14,12},{16,14},{18,16},{20... | collective-permute-start | bytes 3145736 | tf_op jit(solution)/shard_map/ppermute | solution.py:24
  61.2 51.1 %collective-permute-start = (bf16[2,1024,256]{2,1,0:T(8,128)(2,1)}, bf16[2,1024,256]{2,1,0:T(8,128)(2,1)}, u32[]{:S(2)}, u32[]{:S(2)}) collective-permute-start(bf16[2,1024,256]{2,1,0:T(8,128)(2,1)} %pad_maximum_fusion.3), channel_id=1, source_target_pairs={{0,2},{2,4},{4,6},{6,8},{8,10},{10,12},{12,14},{14,16},{16,18},{18... | collective-permute-start | bytes 3145736 | tf_op jit(solution)/shard_map/ppermute | solution.py:22
  94.8 17.5 %copy-start.2 = (bf16[1,1024,256]{2,1,0:T(8,128)(2,1)S(1)}, bf16[1,1024,256]{2,1,0:T(8,128)(2,1)}, u32[]{:S(2)}) copy-start(bf16[1,1024,256]{2,1,0:T(8,128)(2,1)} %copy-done.1) | copy-start | bytes 1572868
  94.8 17.5 %copy-start.4 = (bf16[1,1024,256]{2,1,0:T(8,128)(2,1)S(1)}, bf16[1,1024,256]{2,1,0:T(8,128)(2,1)}, u32[]{:S(2)}) copy-start(bf16[1,1024,256]{2,1,0:T(8,128)(2,1)} %copy-done.3) | copy-start | bytes 1572868
  114.9 2.2 %copy-start.9 = (bf16[2,1024,256]{2,1,0:T(8,128)(2,1)S(1)}, bf16[2,1024,256]{2,1,0:T(8,128)(2,1)}, u32[]{:S(2)}) copy-start(bf16[2,1024,256]{2,1,0:T(8,128)(2,1)} %subtract_convert_fusion) | copy-start | bytes 3145732
  117.1 3.1 %copy-start.14 = (f32[128,128]{1,0:T(8,128)S(1)}, f32[128,128]{1,0:T(8,128)}, u32[]{:S(2)}) copy-start(f32[128,128]{1,0:T(8,128)} %get-tuple-element.15) | copy-start | bytes 196612
  117.1 3.1 %copy-start.15 = (f32[128,128]{1,0:T(8,128)S(1)}, f32[128,128]{1,0:T(8,128)}, u32[]{:S(2)}) copy-start(f32[128,128]{1,0:T(8,128)} %get-tuple-element.19) | copy-start | bytes 196612
  117.1 3.1 %copy-start.16 = (f32[128,128]{1,0:T(8,128)S(1)}, f32[128,128]{1,0:T(8,128)}, u32[]{:S(2)}) copy-start(f32[128,128]{1,0:T(8,128)} %get-tuple-element.20) | copy-start | bytes 196612
  129.4 6.3 %copy-start.5 = (bf16[1,1024,256]{1,2,0:T(8,128)(2,1)S(1)}, bf16[1,1024,256]{1,2,0:T(8,128)(2,1)}, u32[]{:S(2)}) copy-start(bf16[1,1024,256]{1,2,0:T(8,128)(2,1)} %copy.29) | copy-start | bytes 1572868
  132.5 3.1 %copy-start.10 = (f32[1,1024,128]{1,2,0:T(8,128)S(1)}, f32[1,1024,128]{1,2,0:T(8,128)}, u32[]{:S(2)}) copy-start(f32[1,1024,128]{1,2,0:T(8,128)} %convolution_bitcast_fusion) | copy-start | bytes 1572868
  132.5 3.1 %copy-start.11 = (f32[1,1024,128]{1,2,0:T(8,128)S(1)}, f32[1,1024,128]{1,2,0:T(8,128)}, u32[]{:S(2)}) copy-start(f32[1,1024,128]{1,2,0:T(8,128)} %convolution_bitcast_fusion.1) | copy-start | bytes 1572868
